TPU v7x, 32 devices: a whole 2x2x4 slice. The times are simulated.
32 devices in a mesh: dp: 8 (over y, x, core), ctx: 4 (over z).
Axes of the slice: x: 2, y: 2, z: 4, core: 2. Of those that a mesh axis runs over, the one named last changes fastest.
Arguments:
- tokens: bfloat16 [8, 2048, 960], P('dp', 'ctx'), may hold values from -6 to 6
- cotangent: bfloat16 [8, 2048, 960], P('dp', 'ctx'), may hold values from -6 to 6
- lengths: int32 [8], P('dp'), may hold values from 512 to 2048, as said below
- gate_mask: int32 [8, 2048], P('dp', 'ctx'), may hold values 0 or 1
- block_order: int32 [8], replicated, may hold values from 0 to 7, as said below
- w_query: bfloat16 [921600], P(('dp', 'ctx')), may hold values from -0.1875 to 0.1875
- w_key: bfloat16 [307200], P(('dp', 'ctx')), may hold values from -0.1875 to 0.1875
- w_value: bfloat16 [307200], P(('dp', 'ctx')), may hold values from -0.1875 to 0.1875
- w_out: bfloat16 [921600], P(('dp', 'ctx')), may hold values from -1.5 to 1.5
- w_gate: bfloat16 [2457600], P(('dp', 'ctx')), may hold values from -0.1875 to 0.1875
- w_up: bfloat16 [2457600], P(('dp', 'ctx')), may hold values from -0.1875 to 0.1875
- w_down: bfloat16 [2457600], P(('dp', 'ctx')), may hold values from -0.125 to 0.125
- gain_attn: float32 [960], replicated, may hold values from 0.5 to 1.5
- gain_mlp: float32 [960], replicated, may hold values from 0.5 to 1.5
- w_router: float32 [960], replicated, may hold values from -0.1875 to 0.1875
Outputs:
- out_tokens: bfloat16 [8, 2048, 960], P('dp', 'ctx')
- grad_tokens: bfloat16 [8, 2048, 960], P('dp', 'ctx')
- grad_query: float32 [921600], P(('dp', 'ctx'))
- grad_key: float32 [307200], P(('dp', 'ctx'))
- grad_value: float32 [307200], P(('dp', 'ctx'))
- grad_out: float32 [921600], P(('dp', 'ctx'))
- grad_gate: float32 [2457600], P(('dp', 'ctx'))
- grad_up: float32 [2457600], P(('dp', 'ctx'))
- grad_down: float32 [2457600], P(('dp', 'ctx'))
- grad_gain_attn: float32 [960], replicated
- grad_gain_mlp: float32 [960], replicated
- grad_router: float32 [960], replicated
Inputs may be any that keep to these rules, and one draw needn't show every extreme that they name: `lengths`: every sequence has between 512 and 2048 valid tokens; some sequence has exactly 2048 and some exactly 512. `block_order`: stored blocks 2 c and 2 c + 1 hold causal blocks k and 7 - k, in either order; every causal block appears once.
All inputs are finite; a program needn't handle non-finite values. No bound on the sum of `gate_mask` on one device may be relied on, other than what follows from the above.
Results may differ from a plain program's by a relative error of at most 0.014.
Values may be sent and summed in bfloat16 or wider, within the bound.
No kernel may reach another device: no remote copies, remote signals or barrier semaphores. Data moves between devices by JAX's collectives and lax.ppermute only.
A program may use at most 192 MiB of HBM per device.

v0:
```python
import jax
import jax.numpy as jnp
from jax import lax
from jax.sharding import PartitionSpec as P

HEADS = 15
KV_HEADS = 5
HEAD_DIM = 64
FF = 2560
norm_eps = 1e-05
rope_base = 100000.0
neg_big = -1e30
highest = lax.Precision.HIGHEST


def rms_norm(values_in, gain_vec):
    return (
        values_in
        * lax.rsqrt(jnp.mean(values_in * values_in, axis=-1, keepdims=True) + norm_eps)
        * gain_vec
    )


def rotary(positions, head_width):
    frequency = rope_base ** (-jnp.arange(0, head_width, 2).astype(jnp.float32) / head_width)
    angles = positions.astype(jnp.float32)[:, None] * frequency[None, :]
    return (jnp.cos(angles)[:, None, :], jnp.sin(angles)[:, None, :])


def rotate(tensor, cosine, sine_table):
    half_width = tensor.shape[-1] // 2
    first_half = tensor[..., :half_width]
    second = tensor[..., half_width:]
    return jnp.concatenate(
        [first_half * cosine - second * sine_table, second * cosine + first_half * sine_table],
        axis=-1,
    )


def matmul(left, right):
    return jnp.dot(left, right, preferred_element_type=jnp.float32)


def matmul_left_t(left, right):
    return lax.dot_general(
        left, right, (((0,), (0,)), ((), ())), preferred_element_type=jnp.float32
    )


def matmul_right_t(left, right):
    return lax.dot_general(
        left, right, (((1,), (1,)), ((), ())), preferred_element_type=jnp.float32
    )


def silu_times(gate_proj, up_proj):
    return jax.nn.silu(gate_proj) * up_proj


def per_device(
    tokens,
    cotangent,
    lengths,
    gate_mask,
    block_order,
    w_query,
    w_key,
    w_value,
    w_out,
    w_gate,
    w_up,
    w_down,
    gain_attn,
    gain_mlp,
    w_router,
):
    inputs = tokens[0].astype(jnp.float32)
    row_count = inputs.shape[0]
    model_width = inputs.shape[1]
    head_count = HEADS
    kv_count = KV_HEADS
    head_width = HEAD_DIM
    group_size = head_count // kv_count
    kv_width = kv_count * head_width
    ff_width = FF
    score_scale = head_width ** (-0.5)
    ctx_index = lax.axis_index("ctx")
    block_rows = row_count // 2
    all_pos = (
        block_order[:, None] * block_rows + jnp.arange(block_rows, dtype=jnp.int32)[None, :]
    ).reshape(-1)
    total_rows = all_pos.shape[0]
    own_pos = lax.dynamic_slice_in_dim(all_pos, ctx_index * row_count, row_count)
    seq_length = lengths[0]
    allowed = (all_pos[None, :] <= own_pos[:, None]) & (all_pos < seq_length)[None, :]
    targets = (
        (model_width, model_width),
        (model_width, kv_width),
        (model_width, kv_width),
        (model_width, model_width),
        (model_width, ff_width),
        (model_width, ff_width),
        (ff_width, model_width),
    )
    whole = (
        lax.all_gather(w_query, ("dp", "ctx"), axis=0, tiled=True),
        lax.all_gather(w_key, ("dp", "ctx"), axis=0, tiled=True),
        lax.all_gather(w_value, ("dp", "ctx"), axis=0, tiled=True),
        lax.all_gather(w_out, ("dp", "ctx"), axis=0, tiled=True),
        lax.all_gather(w_gate, ("dp", "ctx"), axis=0, tiled=True),
        lax.all_gather(w_up, ("dp", "ctx"), axis=0, tiled=True),
        lax.all_gather(w_down, ("dp", "ctx"), axis=0, tiled=True),
    )
    weight_query, weight_key, weight_value, weight_out, weight_gate, weight_up, weight_down = tuple(
        (flat_piece.reshape(target) for flat_piece, target in zip(whole, targets))
    )
    cosine, sine_table = rotary(own_pos, head_width)
    normed, norm_back = jax.vjp(rms_norm, inputs, gain_attn)
    normed_b = normed.astype(jnp.bfloat16)
    queries = rotate(
        matmul(normed_b, weight_query).reshape(row_count, head_count, head_width),
        cosine,
        sine_table,
    ).astype(jnp.bfloat16)
    key_local = (
        rotate(
            matmul(normed_b, weight_key).reshape(row_count, kv_count, head_width),
            cosine,
            sine_table,
        )
        .astype(jnp.bfloat16)
        .reshape(row_count, kv_width)
    )
    value_local = matmul(normed_b, weight_value).astype(jnp.bfloat16)
    key_all, value_all = (
        lax.all_gather(key_local, "ctx", axis=0, tiled=True),
        lax.all_gather(value_local, "ctx", axis=0, tiled=True),
    )
    query_heads = queries.reshape(row_count, kv_count, group_size, head_width).transpose(1, 0, 2, 3)

    def split_heads(flat_rows):
        return flat_rows.reshape(total_rows, kv_count, head_width).transpose(1, 0, 2)

    def head_forward(packed):
        query_head, key_head, value_head = packed
        raw_scores = (
            jnp.einsum("qgd,kd->gqk", query_head, key_head, preferred_element_type=jnp.float32)
            * score_scale
        )
        raw_scores = jnp.where(allowed[None], raw_scores, neg_big)
        top_score = jnp.max(raw_scores, axis=-1, keepdims=True)
        expo = jnp.exp(raw_scores - top_score)
        totals = jnp.sum(expo, axis=-1, keepdims=True)
        probs = (expo / totals).astype(jnp.bfloat16)
        head_out = jnp.einsum("gqk,kd->qgd", probs, value_head, preferred_element_type=jnp.float32)
        return (head_out, top_score[..., 0] + jnp.log(totals[..., 0]))

    head_outs, log_totals = lax.map(
        head_forward, (query_heads, split_heads(key_all), split_heads(value_all))
    )
    mixed_b = head_outs.transpose(1, 0, 2, 3).reshape(row_count, model_width).astype(jnp.bfloat16)
    attn_out = matmul(mixed_b, weight_out)
    middle = inputs + attn_out
    normed_mlp, mlp_norm_back = jax.vjp(rms_norm, middle, gain_mlp)
    normed_mlp_b = normed_mlp.astype(jnp.bfloat16)
    gate_proj = matmul(normed_mlp_b, weight_gate)
    up_proj = matmul(normed_mlp_b, weight_up)
    hidden_f, silu_back = jax.vjp(silu_times, gate_proj, up_proj)
    hidden = hidden_f.astype(jnp.bfloat16)
    mlp_out = matmul(hidden, weight_down)
    branch = attn_out + mlp_out
    router_gate = jax.nn.sigmoid(jnp.dot(inputs, w_router, precision=highest))
    gate_bits = gate_mask[0].astype(jnp.float32)
    chosen = gate_bits * router_gate
    result = (inputs + chosen[:, None] * branch).astype(jnp.bfloat16)
    usable = (own_pos < seq_length).astype(jnp.float32)
    grad_result = cotangent[0].astype(jnp.float32) * usable[:, None]
    grad_branch = grad_result * chosen[:, None]
    grad_logit = (
        gate_bits * jnp.sum(grad_result * branch, axis=-1) * router_gate * (1.0 - router_gate)
    )
    grad_router = jnp.dot(grad_logit, inputs, precision=highest)
    grad_inputs = grad_result + grad_logit[:, None] * w_router[None, :]
    grad_mlp_b = grad_branch.astype(jnp.bfloat16)
    grad_w_down = matmul_left_t(hidden, grad_mlp_b)
    grad_hidden = matmul_right_t(grad_mlp_b, weight_down)
    grad_gate_f, grad_up_f = silu_back(grad_hidden)
    grad_gate_b = grad_gate_f.astype(jnp.bfloat16)
    grad_up_b = grad_up_f.astype(jnp.bfloat16)
    grad_w_gate = matmul_left_t(normed_mlp_b, grad_gate_b)
    grad_w_up = matmul_left_t(normed_mlp_b, grad_up_b)
    grad_normed_mlp = matmul_right_t(grad_gate_b, weight_gate) + matmul_right_t(
        grad_up_b, weight_up
    )
    grad_middle, grad_gain_mlp = mlp_norm_back(grad_normed_mlp)
    grad_inputs = grad_inputs + grad_middle
    grad_attn_b = (grad_branch + grad_middle).astype(jnp.bfloat16)
    grad_w_out = matmul_left_t(mixed_b, grad_attn_b)
    grad_mixed = matmul_right_t(grad_attn_b, weight_out).astype(jnp.bfloat16)
    grad_heads = grad_mixed.reshape(row_count, kv_count, group_size, head_width).transpose(
        1, 0, 2, 3
    )

    def head_backward(packed):
        query_head, key_head, value_head, grad_head, log_head = packed
        raw_scores = (
            jnp.einsum("qgd,kd->gqk", query_head, key_head, preferred_element_type=jnp.float32)
            * score_scale
        )
        raw_scores = jnp.where(allowed[None], raw_scores, neg_big)
        probs = jnp.exp(raw_scores - log_head[..., None])
        grad_probs = jnp.einsum(
            "qgd,kd->gqk", grad_head, value_head, preferred_element_type=jnp.float32
        )
        row_delta = jnp.sum(probs * grad_probs, axis=-1, keepdims=True)
        grad_scores = (probs * (grad_probs - row_delta)).astype(jnp.bfloat16)
        grad_q = (
            jnp.einsum("gqk,kd->qgd", grad_scores, key_head, preferred_element_type=jnp.float32)
            * score_scale
        )
        grad_k = (
            jnp.einsum("gqk,qgd->kd", grad_scores, query_head, preferred_element_type=jnp.float32)
            * score_scale
        )
        grad_v = jnp.einsum(
            "gqk,qgd->kd", probs.astype(jnp.bfloat16), grad_head, preferred_element_type=jnp.float32
        )
        return (grad_q, grad_k, grad_v)

    grad_q_heads, grad_k_heads, grad_v_heads = lax.map(
        head_backward,
        (query_heads, split_heads(key_all), split_heads(value_all), grad_heads, log_totals),
    )
    grad_keys_all = grad_k_heads.transpose(1, 0, 2).reshape(total_rows, kv_width)
    grad_values_all = grad_v_heads.transpose(1, 0, 2).reshape(total_rows, kv_width)
    own_grad_keys, own_grad_values = (
        lax.psum_scatter(grad_keys_all, "ctx", scatter_dimension=0, tiled=True),
        lax.psum_scatter(grad_values_all, "ctx", scatter_dimension=0, tiled=True),
    )
    grad_query_b = (
        rotate(
            grad_q_heads.transpose(1, 0, 2, 3).reshape(row_count, head_count, head_width),
            cosine,
            -sine_table,
        )
        .astype(jnp.bfloat16)
        .reshape(row_count, model_width)
    )
    grad_key_b = (
        rotate(own_grad_keys.reshape(row_count, kv_count, head_width), cosine, -sine_table)
        .astype(jnp.bfloat16)
        .reshape(row_count, kv_width)
    )
    grad_value_b = own_grad_values.astype(jnp.bfloat16)
    grad_w_query = matmul_left_t(normed_b, grad_query_b)
    grad_w_key = matmul_left_t(normed_b, grad_key_b)
    grad_w_value = matmul_left_t(normed_b, grad_value_b)
    grad_normed = (
        matmul_right_t(grad_query_b, weight_query)
        + matmul_right_t(grad_key_b, weight_key)
        + matmul_right_t(grad_value_b, weight_value)
    )
    grad_in_norm, grad_gain_attn = norm_back(grad_normed)
    grad_inputs = grad_inputs + grad_in_norm
    query_shard, key_shard, value_shard, out_shard, gate_shard, up_shard, down_shard = (
        lax.psum_scatter(grad_w_query.reshape(-1), ("dp", "ctx"), scatter_dimension=0, tiled=True),
        lax.psum_scatter(grad_w_key.reshape(-1), ("dp", "ctx"), scatter_dimension=0, tiled=True),
        lax.psum_scatter(grad_w_value.reshape(-1), ("dp", "ctx"), scatter_dimension=0, tiled=True),
        lax.psum_scatter(grad_w_out.reshape(-1), ("dp", "ctx"), scatter_dimension=0, tiled=True),
        lax.psum_scatter(grad_w_gate.reshape(-1), ("dp", "ctx"), scatter_dimension=0, tiled=True),
        lax.psum_scatter(grad_w_up.reshape(-1), ("dp", "ctx"), scatter_dimension=0, tiled=True),
        lax.psum_scatter(grad_w_down.reshape(-1), ("dp", "ctx"), scatter_dimension=0, tiled=True),
    )
    gain_attn_sum, gain_mlp_sum, router_sum = lax.psum(
        (grad_gain_attn, grad_gain_mlp, grad_router), ("dp", "ctx")
    )
    return (
        result[None],
        grad_inputs.astype(jnp.bfloat16)[None],
        query_shard,
        key_shard,
        value_shard,
        out_shard,
        gate_shard,
        up_shard,
        down_shard,
        gain_attn_sum,
        gain_mlp_sum,
        router_sum,
    )


def solution(mesh):
    placed = (
        P("dp", "ctx", None),
        P("dp", "ctx", None),
        P("dp"),
        P("dp", "ctx"),
        P(),
        P(("dp", "ctx")),
        P(("dp", "ctx")),
        P(("dp", "ctx")),
        P(("dp", "ctx")),
        P(("dp", "ctx")),
        P(("dp", "ctx")),
        P(("dp", "ctx")),
        P(),
        P(),
        P(),
    )
    return jax.shard_map(
        per_device,
        mesh=mesh,
        in_specs=placed,
        out_specs=(
            P("dp", "ctx", None),
            P("dp", "ctx", None),
            P(("dp", "ctx")),
            P(("dp", "ctx")),
            P(("dp", "ctx")),
            P(("dp", "ctx")),
            P(("dp", "ctx")),
            P(("dp", "ctx")),
            P(("dp", "ctx")),
            P(),
            P(),
            P(),
        ),
        check_vma=False,
    )
```

profile of v0, /device:TPU:0, one launch (start us, length us, event | category | flops | bytes accessed | tf_op | source)
XLA Modules:
  0.0 1370.1 jit_solution(13818543416422502174)
XLA Ops:
  9.6 84.9 %all-gather = bf16[32,1,9600]{2,1,0:T(2,128)(2,1)S(1)} all-gather(bf16[1,1,9600]{2,1,0:T(2,128)(2,1)S(1)} %reshape.399), channel_id=1, replica_groups=mesh['dp'=8,'ctx'=4] {'dp','ctx'}, dimensions={0}, use_global_device_ids=true | all-gather | bytes 633600 | tf_op jit(solution)/shard_map/all_gather | solution.py:108
  101.7 81.8 %all-gather.1 = bf16[32,1,9600]{2,1,0:T(2,128)(2,1)S(1)} all-gather(bf16[1,1,9600]{2,1,0:T(2,128)(2,1)S(1)} %reshape.401), channel_id=1, replica_groups=mesh['dp'=8,'ctx'=4] {'dp','ctx'}, dimensions={0}, use_global_device_ids=true | all-gather | bytes 633600 | tf_op jit(solution)/shard_map/all_gather | solution.py:107
  196.9 40.8 %reduce.2 = bf16[32,28800]{1,0:T(8,128)(2,1)} reduce(bf16[32,1,28800]{2,1,0:T(2,128)(2,1)} %all-gather.22.cloned.1.call-done, bf16[]{:T(256)} %constant.108), dimensions={1}, to_apply=%all-gather.2.reduce_sub_computation | reduce | bytes 3686402 | tf_op jit(solution)/shard_map/all_gather | solution.py:106
  247.5 75.0 %while.30 = (s32[]{:T(128)}, bf16[5,512,3,64]{1,3,2,0:T(8,128)(2,1)}, f32[5,3,512]{2,1,0:T(4,128)S(1)}, bf16[5,2048,64]{1,2,0:T(8,128)(2,1)}, bf16[5,2048,64]{1,...) while((s32[]{:T(128)}, ...), condition=%wide.region_4.5_spmd.clone.clone, body=%wide.region_1.4_spmd.clone.sunk.clone | while | flops 845150720 | bytes 47321220 | solution.py:158
  322.6 39.5 %reduce.3 = bf16[32,28800]{1,0:T(8,128)(2,1)S(1)} reduce(bf16[32,1,28800]{2,1,0:T(2,128)(2,1)} %all-gather.24.cloned.1.call-done, bf16[]{:T(256)} %constant.108), dimensions={1}, to_apply=%all-gather.3.reduce_sub_computation | reduce | bytes 3686402 | tf_op jit(solution)/shard_map/all_gather | solution.py:109
  369.9 10.3 reshape.383
  380.3 35.4 %all-gather.18.cloned.1.call-done = bf16[2457600]{0:T(1024)(128)(2,1)} async-done(((bf16[76800]{0:T(1024)(128)(2,1)}), bf16[2457600]{0:T(1024)(128)(2,1)}) %all-gather.18.cloned.1.call-update) | async-done | bytes 4915216 | tf_op jit(solution)/shard_map/all_gather | solution.py:111
  415.6 10.0 reshape.384
  425.6 7.2 fusion.122
  437.5 43.6 %all-gather.20.cloned.1.call-done = bf16[2457600]{0:T(1024)(128)(2,1)} async-done(((bf16[76800]{0:T(1024)(128)(2,1)}), bf16[2457600]{0:T(1024)(128)(2,1)}) %all-gather.20.cloned.1.call-update) | async-done | bytes 4915216 | tf_op jit(solution)/shard_map/all_gather | solution.py:112
  481.1 9.5 reshape.385
  490.6 9.5 multiply_convert_fusion
  500.1 7.1 fusion.124
  520.9 145.6 %while.31 = (s32[]{:T(128)}, f32[5,512,3,64]{1,3,2,0:T(8,128)S(1)}, f32[5,2048,64]{1,2,0:T(8,128)}, f32[5,2048,64]{1,2,0:T(8,128)}, bf16[5,2048,64]{1,2,0:T(8,12...) while((s32[]{:T(128)}, f32[5,512,3,64]{1,3,2,0:T(8,128)S(1)}, ...), condition=%wide.region_10.11_spmd.clone.clone, body=%wide.region_8.10_spmd.clone.sunk.clone | while | flops 2062776832 | bytes 101645440 | solution.py:230
  525.4 7.7 fusion.215
  533.2 6.9 fusion.216
  554.5 7.7 fusion.215
  562.2 6.9 fusion.216
  583.6 7.7 fusion.215
  591.3 6.9 fusion.216
  612.7 7.7 fusion.215
  620.4 6.9 fusion.216
  641.8 7.7 fusion.215
  687.5 7.0 fusion.126
  694.5 11.0 reshape.395
  705.5 7.0 fusion.127
  712.5 11.1 reshape.396
  723.6 7.6 fusion.91
  731.2 13.3 reshape.397
  748.3 23.1 %reduce-scatter.5.cloned.1.call-done = f32[512,320]{0,1:T(8,128)} async-done(((f32[2048,320]{0,1:T(8,128)}), f32[512,320]{0,1:T(8,128)}) %reduce-scatter.5.cloned.1.call-update) | async-done | bytes 655376 | tf_op jit(solution)/shard_map/reduce_scatter | solution.py:238
  782.9 41.8 %all-reduce.7 = (f32[960]{0:T(1024)}, f32[960]{0:T(1024)}, f32[960]{0:T(1024)}) all-reduce(f32[960]{0:T(1024)S(1)} %get-tuple-element.163, f32[960]{0:T(1024)S(1)} %copy-done.49, f32[960]{0:T(1024)S(1)} %bitcast.380), channel_id=1, replica_groups=mesh['dp'=8,'ctx'=4] {'dp','ctx'}, use_global_device_ids=true, to_apply=%region_22.23 | all-reduce | flops 2880 | bytes 23040 | tf_op jit(solution)/shard_map/psum | solution.py:274
  828.8 522.8 %all-reduce.11.cloned.1.call-done = (f32[921600]{0:T(1024)}, f32[307200]{0:T(1024)}, f32[307200]{0:T(1024)}, f32[921600]{0:T(1024)}, f32[2457600]{0:T(1024)}, /*index=5*/f32[2457600]{0:T(1024)}, f32[2457600]{0:T(1024)}) async-done(((f32[921600]{0:T(1024)}, f32[307200]{0:T(1024)}, f32[307200]{0:T(1024)}, f32[921600]{0:T(1024)}, f32[2457600]{0:T(1024)}, /*index=5*/f32[2457600]{0:T(1024)}, f32[2457600]{0:T(1024)}), ...) | async-done | bytes 39321616
  (284 shorter events, 263.0 us)
Async XLA Ops:
  7.2 189.7 %all-gather.22.cloned.1.call-start = ((), (), s32[]{:S(2)}) async-start(), calls=%async_computation.9 | async-start | bytes 3801600 | tf_op jit(solution)/shard_map/all_gather | solution.py:106
  8.8 238.8 %all-gather.12.cloned.1.call-start = ((), (), s32[]{:S(2)}) async-start(), calls=%async_computation.2 | async-start | bytes 1638400 | tf_op jit(solution)/shard_map/all_gather | solution.py:137
  9.6 89.4 %copy-start.1 = (bf16[1,512,960]{1,2,0:T(8,128)(2,1)S(1)}, bf16[1,512,960]{1,2,0:T(8,128)(2,1)}, u32[]{:S(2)}) copy-start(bf16[1,512,960]{1,2,0:T(8,128)(2,1)} %param.19) | copy-start | bytes 2949124
  99.3 144.0 %copy-start.30 = (f32[512]{0:T(512)}, f32[512]{0:T(512)S(1)}, u32[]{:S(2)}) copy-start(f32[512]{0:T(512)S(1)} %fusion.119) | copy-start | bytes 6148
  100.8 146.7 %all-gather.14.cloned.1.call-start = ((), (), s32[]{:S(2)}) async-start(), calls=%async_computation.3 | async-start | bytes 1638400 | tf_op jit(solution)/shard_map/all_gather | solution.py:136
  189.9 56.3 %copy-start.20 = (f32[512,32]{0,1:T(8,128)}, f32[512,32]{0,1:T(8,128)S(1)}, u32[]{:S(2)}) copy-start(f32[512,32]{0,1:T(8,128)S(1)} %get-tuple-element.239) | copy-start | bytes 196612
  191.4 131.2 %all-gather.24.cloned.1.call-start = ((), (), s32[]{:S(2)}) async-start(), calls=%async_computation.10 | async-start | bytes 3801600 | tf_op jit(solution)/shard_map/all_gather | solution.py:109
  192.2 177.7 %all-gather.16.cloned.1.call-start = ((), (), s32[]{:S(2)}) async-start(), calls=%async_computation.4 | async-start | bytes 5068800 | tf_op jit(solution)/shard_map/all_gather | solution.py:110
  192.8 222.8 %all-gather.18.cloned.1.call-start = ((), (), s32[]{:S(2)}) async-start(), calls=%async_computation.5 | async-start | bytes 5068800 | tf_op jit(solution)/shard_map/all_gather | solution.py:111
  193.4 287.7 %all-gather.20.cloned.1.call-start = ((), (), s32[]{:S(2)}) async-start(), calls=%async_computation.6 | async-start | bytes 5068800 | tf_op jit(solution)/shard_map/all_gather | solution.py:112
  194.1 550.4 %reduce-scatter.3.cloned.1.call-start = ((), (), s32[]{:S(2)}) async-start(), calls=%async_computation.7 | async-start | bytes 3276800 | tf_op jit(solution)/shard_map/reduce_scatter | solution.py:237
  195.7 41.9 %copy-start.39 = (f32[1,512]{1,0:T(1,128)}, f32[1,512]{1,0:T(1,128)S(1)}, u32[]{:S(2)}) copy-start(f32[1,512]{1,0:T(1,128)S(1)} %convert_element_type.146) | copy-start | bytes 6148
  196.2 41.4 %copy-start.37 = (f32[1,512]{1,0:T(1,128)}, f32[1,512]{1,0:T(1,128)S(1)}, u32[]{:S(2)}) copy-start(f32[1,512]{1,0:T(1,128)S(1)} %fusion.107) | copy-start | bytes 6148
  368.3 145.4 %copy-start.33 = (f32[512]{0:T(512)}, f32[512]{0:T(512)S(1)}, u32[]{:S(2)}) copy-start(f32[512]{0:T(512)S(1)} %fusion.120) | copy-start | bytes 6148
  369.9 63.0 %copy-start.5 = (bf16[512,960]{0,1:T(8,128)(2,1)}, bf16[512,960]{0,1:T(8,128)(2,1)S(1)}, u32[]{:S(2)}) copy-start(bf16[512,960]{0,1:T(8,128)(2,1)S(1)} %multiply_convert_fusion.2) | copy-start | bytes 2949124
  425.6 7.3 copy-start.4
  437.5 53.1 %copy-start.22 = (bf16[1,512,960]{1,2,0:T(8,128)(2,1)S(1)}, bf16[1,512,960]{1,2,0:T(8,128)(2,1)}, u32[]{:S(2)}) copy-start(bf16[1,512,960]{1,2,0:T(8,128)(2,1)} %param.20) | copy-start | bytes 2949124
  437.5 53.1 %copy-start.45 = (f32[512]{0:T(512)S(1)}, f32[512]{0:T(512)}, u32[]{:S(2)}) copy-start(f32[512]{0:T(512)} %get-tuple-element.217) | copy-start | bytes 6148
  437.5 53.1 %copy-start.50 = (f32[512]{0:T(512)S(1)}, f32[512]{0:T(512)}, u32[]{:S(2)}) copy-start(f32[512]{0:T(512)} %fusion.121) | copy-start | bytes 6148
  500.1 13.5 copy-start.56
  500.1 13.5 slice-start
  666.6 104.9 %reduce-scatter.5.cloned.1.call-start = ((), (), s32[]{:S(2)}) async-start(), calls=%async_computation.8 | async-start | bytes 3276800 | tf_op jit(solution)/shard_map/reduce_scatter | solution.py:238
  667.3 684.4 %all-reduce.11.cloned.1.call-start = ((), (), s32[]{:S(2)}) async-start(), calls=%async_computation.11 | async-start | bytes 78643200
  712.5 11.1 copy-start.23
  712.5 11.1 copy-start.46
  712.5 11.1 copy-start.51
  780.4 44.2 %copy-start.36 = (f32[512]{0:T(512)S(1)}, f32[512]{0:T(512)}, u32[]{:S(2)}) copy-start(f32[512]{0:T(512)} %copy-done.35) | copy-start | bytes 6148
  780.4 44.3 %copy-start.9 = (f32[512,960]{0,1:T(8,128)S(1)}, f32[512,960]{0,1:T(8,128)}, u32[]{:S(2)}) copy-start(f32[512,960]{0,1:T(8,128)} %copy-done.7) | copy-start | bytes 5898244
  780.4 44.3 %copy-start.34 = (f32[512]{0:T(512)S(1)}, f32[512]{0:T(512)}, u32[]{:S(2)}) copy-start(f32[512]{0:T(512)} %copy-done.33) | copy-start | bytes 6148
  780.4 44.3 %copy-start.42 = (f32[960]{0:T(1024)S(1)}, f32[960]{0:T(1024)}, u32[]{:S(2)}) copy-start(f32[960]{0:T(1024)} %param.33) | copy-start | bytes 11524
  780.4 44.3 %copy-start.44 = (f32[960]{0:T(1024)S(1)}, f32[960]{0:T(1024)}, u32[]{:S(2)}) copy-start(f32[960]{0:T(1024)} %param.32) | copy-start | bytes 11524
  780.5 44.3 %copy-start.48 = (f32[512]{0:T(512)S(1)}, f32[512]{0:T(512)}, u32[]{:S(2)}) copy-start(f32[512]{0:T(512)} %copy-done.47) | copy-start | bytes 6148
  (43 other events, 136.7 us)
Sparse Core Ops, SparseCore 0:
  11.4 65.3 all-gather.21
  100.9 36.9 all-gather.11
  191.5 29.9 all-gather.13
  224.8 59.7 all-gather.23
  287.3 62.9 all-gather.15
  353.0 62.5 all-gather.17
  418.5 62.6 all-gather.19
  666.7 50.5 reduce-scatter.2
  719.6 51.7 reduce-scatter.4
  777.7 573.9 all-reduce.10
where the time goes:
time: 1380 us; the launch traced here: 1370 us
  waiting for transfers between devices  627 us (45%)
  matrix products  238 us (17%)
  blocking collectives  209 us (15%)
  other arithmetic  169 us (12%)
  local copies, waits for them, and re-layouts  110 us (8%)
  between operations  15.8 us (1%)
    unnamed x11, waiting for transfers between devices  525 us
    all_gather x1, blocking collectives, per_device(): lax.all_gather(w_value, ('dp', 'ctx'), axis=0, tiled=True)  84.9 us
    all_gather x1, blocking collectives, per_device(): lax.all_gather(w_key, ('dp', 'ctx'), axis=0, tiled=True)  81.8 us
    all_gather x1, waiting for transfers between devices, per_device(): lax.all_gather(w_down, ('dp', 'ctx'), axis=0, tiled=True)  43.6 us
    psum x1, blocking collectives, per_device(): lax.psum((grad_gain_attn, grad_gain_mlp, grad_router), ('dp', 'ctx'))  41.8 us
    all_gather x1, other arithmetic, per_device(): lax.all_gather(w_query, ('dp', 'ctx'), axis=0, tiled=True)  40.8 us
    all_gather x1, other arithmetic, per_device(): lax.all_gather(w_out, ('dp', 'ctx'), axis=0, tiled=True)  39.5 us
    dot_general x5, matrix products, head_backward(): jnp.einsum('qgd,kd->gqk', grad_head, value_head, preferred_element_type=j...  38.5 us
  transfers between devices with their start and end apart: 10, of which 4 were waited for; matrix products, arithmetic and copies ran while one was open for 23% of the time, Pallas kernels for 0%

commit v1 on v0

--- a/solution.py
+++ b/solution.py
@@ -102,9 +102,32 @@
         (model_width, ff_width),
         (ff_width, model_width),
     )
+
+    def get_chunk_in(message):
+        tile_out, raw_out, block_out = (
+            lax.axis_size(("dp", "ctx")),
+            lax.axis_index(("dp", "ctx")),
+            message.shape[0],
+        )
+        v1, n_now = (message, 1)
+        while n_now < tile_out:
+            v1 = jnp.concatenate(
+                [
+                    v1,
+                    lax.ppermute(
+                        v1,
+                        ("dp", "ctx"),
+                        tuple(((k0, (k0 - n_now) % tile_out) for k0 in range(tile_out))),
+                    ),
+                ],
+                axis=0,
+            )
+            n_now = 2 * n_now
+        return jnp.roll(v1, shift=raw_out * block_out, axis=0)
+
     whole = (
         lax.all_gather(w_query, ("dp", "ctx"), axis=0, tiled=True),
-        lax.all_gather(w_key, ("dp", "ctx"), axis=0, tiled=True),
+        get_chunk_in(w_key),
         lax.all_gather(w_value, ("dp", "ctx"), axis=0, tiled=True),
         lax.all_gather(w_out, ("dp", "ctx"), axis=0, tiled=True),
         lax.all_gather(w_gate, ("dp", "ctx"), axis=0, tiled=True),

time: 1380 us -> 1340 us (0.971)
  blocking collectives: 209 us -> 122 us
  local copies, waits for them, and re-layouts: 110 us -> 130 us
  waiting for transfers between devices: 627 us -> 643 us
    all_gather x1 -> x0, blocking collectives: 81.8 us -> none  [per_device(): lax.all_gather(w_key, ('dp', 'ctx'), axis=0, tiled=True)]
    unnamed x132 -> x145, local copies, waits for them, and re-layouts: 18.7 us -> 36.1 us
  transfers between devices with their start and end apart: 10 -> 15, of which waited for: 4 -> 7; matrix products, arithmetic and copies ran while one was open for 23% -> 25% of each run, Pallas kernels for 0% -> 0%
where the time goes in v1:
time: 1340 us; the launch traced here: 1320 us
  waiting for transfers between devices  643 us (48%)
  matrix products  238 us (18%)
  other arithmetic  166 us (12%)
  local copies, waits for them, and re-layouts  130 us (10%)
  blocking collectives  122 us (9%)
  between operations  16.1 us (1%)
    unnamed x11, waiting for transfers between devices  525 us
    all_gather x1, blocking collectives, per_device(): lax.all_gather(w_value, ('dp', 'ctx'), axis=0, tiled=True)  80.4 us
    all_gather x1, waiting for transfers between devices, per_device(): lax.all_gather(w_down, ('dp', 'ctx'), axis=0, tiled=True)  43.6 us
    psum x1, blocking collectives, per_device(): lax.psum((grad_gain_attn, grad_gain_mlp, grad_router), ('dp', 'ctx'))  41.8 us
    all_gather x1, other arithmetic, per_device(): lax.all_gather(w_query, ('dp', 'ctx'), axis=0, tiled=True)  40.8 us
    all_gather x1, other arithmetic, per_device(): lax.all_gather(w_out, ('dp', 'ctx'), axis=0, tiled=True)  39.5 us
    dot_general x5, matrix products, head_backward(): jnp.einsum('qgd,kd->gqk', grad_head, value_head, preferred_element_type=j...  38.5 us
    all_gather x1, waiting for transfers between devices, per_device(): lax.all_gather(w_up, ('dp', 'ctx'), axis=0, tiled=True)  38.3 us
  transfers between devices with their start and end apart: 15, of which 7 were waited for; matrix products, arithmetic and copies ran while one was open for 25% of the time, Pallas kernels for 0%

profile of v1, /device:TPU:0, one launch (start us, length us, event | category | flops | bytes accessed | tf_op | source)
XLA Modules:
  0.0 1324.2 jit_solution(10087319805093206161)
XLA Ops:
  17.5 80.4 %all-gather = bf16[32,1,9600]{2,1,0:T(2,128)(2,1)S(1)} all-gather(bf16[1,1,9600]{2,1,0:T(2,128)(2,1)S(1)} %reshape.399), channel_id=1, replica_groups=mesh['dp'=8,'ctx'=4] {'dp','ctx'}, dimensions={0}, use_global_device_ids=true | all-gather | bytes 633600 | tf_op jit(solution)/shard_map/all_gather | solution.py:131
  122.0 7.4 collective-permute-done.4
  147.7 40.8 %reduce.1 = bf16[32,28800]{1,0:T(8,128)(2,1)} reduce(bf16[32,1,28800]{2,1,0:T(2,128)(2,1)} %all-gather.21.cloned.1.call-done, bf16[]{:T(256)} %constant.135), dimensions={1}, to_apply=%all-gather.1.reduce_sub_computation | reduce | bytes 3686402 | tf_op jit(solution)/shard_map/all_gather | solution.py:129
  198.3 75.0 %while.30 = (s32[]{:T(128)}, bf16[5,512,3,64]{1,3,2,0:T(8,128)(2,1)}, f32[5,3,512]{2,1,0:T(4,128)S(1)}, bf16[5,2048,64]{1,2,0:T(8,128)(2,1)}, bf16[5,2048,64]{1,...) while((s32[]{:T(128)}, ...), condition=%wide.region_4.5_spmd.clone.clone, body=%wide.region_1.4_spmd.clone.sunk.clone | while | flops 845150720 | bytes 47321220 | solution.py:181
  273.4 39.5 %reduce.2 = bf16[32,28800]{1,0:T(8,128)(2,1)S(1)} reduce(bf16[32,1,28800]{2,1,0:T(2,128)(2,1)} %all-gather.23.cloned.1.call-done, bf16[]{:T(256)} %constant.135), dimensions={1}, to_apply=%all-gather.2.reduce_sub_computation | reduce | bytes 3686402 | tf_op jit(solution)/shard_map/all_gather | solution.py:132
  320.7 10.3 reshape.383
  331.0 38.3 %all-gather.17.cloned.1.call-done = bf16[2457600]{0:T(1024)(128)(2,1)} async-done(((bf16[76800]{0:T(1024)(128)(2,1)}), bf16[2457600]{0:T(1024)(128)(2,1)}) %all-gather.17.cloned.1.call-update) | async-done | bytes 4915216 | tf_op jit(solution)/shard_map/all_gather | solution.py:134
  369.4 10.0 reshape.384
  379.3 7.2 fusion.123
  391.3 43.6 %all-gather.19.cloned.1.call-done = bf16[2457600]{0:T(1024)(128)(2,1)} async-done(((bf16[76800]{0:T(1024)(128)(2,1)}), bf16[2457600]{0:T(1024)(128)(2,1)}) %all-gather.19.cloned.1.call-update) | async-done | bytes 4915216 | tf_op jit(solution)/shard_map/all_gather | solution.py:135
  434.8 9.5 reshape.385
  444.4 9.5 multiply_convert_fusion
  453.9 7.1 fusion.125
  474.6 145.8 %while.31 = (s32[]{:T(128)}, f32[5,512,3,64]{1,3,2,0:T(8,128)S(1)}, f32[5,2048,64]{1,2,0:T(8,128)}, f32[5,2048,64]{1,2,0:T(8,128)}, bf16[5,2048,64]{1,2,0:T(8,12...) while((s32[]{:T(128)}, f32[5,512,3,64]{1,3,2,0:T(8,128)S(1)}, ...), condition=%wide.region_10.11_spmd.clone.clone, body=%wide.region_8.10_spmd.clone.sunk.clone | while | flops 2062776832 | bytes 101645440 | solution.py:253
  479.2 7.7 fusion.215
  486.9 6.9 fusion.216
  508.3 7.7 fusion.215
  516.0 6.9 fusion.216
  537.4 7.7 fusion.215
  545.1 6.9 fusion.216
  566.6 7.7 fusion.215
  595.7 7.7 fusion.215
  603.4 6.9 fusion.216
  641.3 7.1 fusion.127
  648.4 11.0 reshape.395
  659.3 7.1 fusion.128
  666.4 11.1 reshape.396
  677.5 7.5 fusion.91
  685.0 13.3 %reshape.397 = f32[2457600]{0:T(1024)} reshape(f32[2560,960]{1,0:T(8,128)} %fusion.91) | data formatting | bytes 19660800 | tf_op jit(solution)/shard_map/reshape | solution.py:295
  702.0 23.3 %reduce-scatter.5.cloned.1.call-done = f32[512,320]{0,1:T(8,128)} async-done(((f32[2048,320]{0,1:T(8,128)}), f32[512,320]{0,1:T(8,128)}) %reduce-scatter.5.cloned.1.call-update) | async-done | bytes 655376 | tf_op jit(solution)/shard_map/reduce_scatter | solution.py:261
  736.7 41.8 %all-reduce.7 = (f32[960]{0:T(1024)}, f32[960]{0:T(1024)}, f32[960]{0:T(1024)}) all-reduce(f32[960]{0:T(1024)S(1)} %get-tuple-element.163, f32[960]{0:T(1024)S(1)} %copy-done.49, f32[960]{0:T(1024)S(1)} %bitcast.380), channel_id=1, replica_groups=mesh['dp'=8,'ctx'=4] {'dp','ctx'}, use_global_device_ids=true, to_apply=%region_22.23 | all-reduce | flops 2880 | bytes 23040 | tf_op jit(solution)/shard_map/psum | solution.py:297
  782.6 522.9 %all-reduce.11.cloned.1.call-done = (f32[921600]{0:T(1024)}, f32[307200]{0:T(1024)}, f32[307200]{0:T(1024)}, f32[921600]{0:T(1024)}, f32[2457600]{0:T(1024)}, /*index=5*/f32[2457600]{0:T(1024)}, f32[2457600]{0:T(1024)}) async-done(((f32[921600]{0:T(1024)}, f32[307200]{0:T(1024)}, f32[307200]{0:T(1024)}, f32[921600]{0:T(1024)}, f32[2457600]{0:T(1024)}, /*index=5*/f32[2457600]{0:T(1024)}, f32[2457600]{0:T(1024)}), ...) | async-done | bytes 39321616
  (313 shorter events, 292.8 us)
Async XLA Ops:
  7.2 140.5 %all-gather.21.cloned.1.call-start = ((), (), s32[]{:S(2)}) async-start(), calls=%async_computation.9 | async-start | bytes 3801600 | tf_op jit(solution)/shard_map/all_gather | solution.py:129
  8.8 189.6 %all-gather.11.cloned.1.call-start = ((), (), s32[]{:S(2)}) async-start(), calls=%async_computation.2 | async-start | bytes 1638400 | tf_op jit(solution)/shard_map/all_gather | solution.py:160
  8.8 93.6 %collective-permute-start = (bf16[9600]{0:T(1024)(128)(2,1)}, bf16[9600]{0:T(1024)(128)(2,1)S(1)}, u32[]{:S(2)}, u32[]{:S(2)}) collective-permute-start(bf16[9600]{0:T(1024)(128)(2,1)} %param.25), channel_id=1, source_target_pairs={{0,31},{1,0},{2,1},{3,2},{4,3},{5,4},{6,5},{7,6},{8,7},{9,8},{10,9... | collective-permute-start | bytes 57608 | tf_op jit(solution)/shard_map/ppermute | solution.py:117
  17.5 84.9 %copy-start.35 = (f32[512]{0:T(512)}, f32[512]{0:T(512)S(1)}, u32[]{:S(2)}) copy-start(f32[512]{0:T(512)S(1)} %fusion.84) | copy-start | bytes 6148
  17.5 84.9 %copy-start.26 = (bf16[9600]{0:T(1024)(128)(2,1)S(1)}, bf16[9600]{0:T(1024)(128)(2,1)}, u32[]{:S(2)}) copy-start(bf16[9600]{0:T(1024)(128)(2,1)} %param.25) | copy-start | bytes 57604
  17.5 85.0 %copy-start.1 = (bf16[1,512,960]{1,2,0:T(8,128)(2,1)S(1)}, bf16[1,512,960]{1,2,0:T(8,128)(2,1)}, u32[]{:S(2)}) copy-start(bf16[1,512,960]{1,2,0:T(8,128)(2,1)} %param.19) | copy-start | bytes 2949124
  17.5 85.0 %copy-start.29 = (f32[960]{0:T(1024)S(1)}, f32[960]{0:T(1024)}, u32[]{:S(2)}) copy-start(f32[960]{0:T(1024)} %param.31) | copy-start | bytes 11524
  97.9 96.3 %copy-start.31 = (f32[512]{0:T(512)}, f32[512]{0:T(512)S(1)}, u32[]{:S(2)}) copy-start(f32[512]{0:T(512)S(1)} %fusion.120) | copy-start | bytes 6148
  102.5 4.9 collective-permute-start.1
  104.0 94.3 %all-gather.13.cloned.1.call-start = ((), (), s32[]{:S(2)}) async-start(), calls=%async_computation.3 | async-start | bytes 1638400 | tf_op jit(solution)/shard_map/all_gather | solution.py:159
  107.4 2.1 collective-permute-start.2
  109.6 10.8 collective-permute-start.3
  121.0 8.3 collective-permute-start.4
  122.0 75.0 %copy-start.20 = (f32[512,32]{0,1:T(8,128)}, f32[512,32]{0,1:T(8,128)S(1)}, u32[]{:S(2)}) copy-start(f32[512,32]{0,1:T(8,128)S(1)} %get-tuple-element.241) | copy-start | bytes 196612
  142.3 131.1 %all-gather.23.cloned.1.call-start = ((), (), s32[]{:S(2)}) async-start(), calls=%async_computation.10 | async-start | bytes 3801600 | tf_op jit(solution)/shard_map/all_gather | solution.py:132
  143.1 177.6 %all-gather.15.cloned.1.call-start = ((), (), s32[]{:S(2)}) async-start(), calls=%async_computation.4 | async-start | bytes 5068800 | tf_op jit(solution)/shard_map/all_gather | solution.py:133
  143.7 225.7 %all-gather.17.cloned.1.call-start = ((), (), s32[]{:S(2)}) async-start(), calls=%async_computation.5 | async-start | bytes 5068800 | tf_op jit(solution)/shard_map/all_gather | solution.py:134
  144.2 290.6 %all-gather.19.cloned.1.call-start = ((), (), s32[]{:S(2)}) async-start(), calls=%async_computation.6 | async-start | bytes 5068800 | tf_op jit(solution)/shard_map/all_gather | solution.py:135
  145.0 553.3 %reduce-scatter.3.cloned.1.call-start = ((), (), s32[]{:S(2)}) async-start(), calls=%async_computation.7 | async-start | bytes 3276800 | tf_op jit(solution)/shard_map/reduce_scatter | solution.py:260
  319.1 148.3 %copy-start.33 = (f32[512]{0:T(512)}, f32[512]{0:T(512)S(1)}, u32[]{:S(2)}) copy-start(f32[512]{0:T(512)S(1)} %fusion.121) | copy-start | bytes 6148
  320.7 65.9 %copy-start.5 = (bf16[512,960]{0,1:T(8,128)(2,1)}, bf16[512,960]{0,1:T(8,128)(2,1)S(1)}, u32[]{:S(2)}) copy-start(bf16[512,960]{0,1:T(8,128)(2,1)S(1)} %multiply_convert_fusion.2) | copy-start | bytes 2949124
  391.2 53.1 %copy-start.22 = (bf16[1,512,960]{1,2,0:T(8,128)(2,1)S(1)}, bf16[1,512,960]{1,2,0:T(8,128)(2,1)}, u32[]{:S(2)}) copy-start(bf16[1,512,960]{1,2,0:T(8,128)(2,1)} %param.20) | copy-start | bytes 2949124
  391.3 53.1 %copy-start.45 = (f32[512]{0:T(512)S(1)}, f32[512]{0:T(512)}, u32[]{:S(2)}) copy-start(f32[512]{0:T(512)} %get-tuple-element.217) | copy-start | bytes 6148
  391.3 53.1 %copy-start.50 = (f32[512]{0:T(512)S(1)}, f32[512]{0:T(512)}, u32[]{:S(2)}) copy-start(f32[512]{0:T(512)} %fusion.122) | copy-start | bytes 6148
  620.4 104.9 %reduce-scatter.5.cloned.1.call-start = ((), (), s32[]{:S(2)}) async-start(), calls=%async_computation.8 | async-start | bytes 3276800 | tf_op jit(solution)/shard_map/reduce_scatter | solution.py:261
  621.2 684.4 %all-reduce.11.cloned.1.call-start = ((), (), s32[]{:S(2)}) async-start(), calls=%async_computation.11 | async-start | bytes 78643200
  734.2 44.3 %copy-start.36 = (f32[512]{0:T(512)S(1)}, f32[512]{0:T(512)}, u32[]{:S(2)}) copy-start(f32[512]{0:T(512)} %copy-done.35) | copy-start | bytes 6148
  734.2 44.3 %copy-start.9 = (f32[512,960]{0,1:T(8,128)S(1)}, f32[512,960]{0,1:T(8,128)}, u32[]{:S(2)}) copy-start(f32[512,960]{0,1:T(8,128)} %copy-done.7) | copy-start | bytes 5898244
  734.2 44.3 %copy-start.34 = (f32[512]{0:T(512)S(1)}, f32[512]{0:T(512)}, u32[]{:S(2)}) copy-start(f32[512]{0:T(512)} %copy-done.33) | copy-start | bytes 6148
  734.2 44.3 %copy-start.42 = (f32[960]{0:T(1024)S(1)}, f32[960]{0:T(1024)}, u32[]{:S(2)}) copy-start(f32[960]{0:T(1024)} %param.33) | copy-start | bytes 11524
  734.2 44.3 %copy-start.44 = (f32[960]{0:T(1024)S(1)}, f32[960]{0:T(1024)}, u32[]{:S(2)}) copy-start(f32[960]{0:T(1024)} %param.32) | copy-start | bytes 11524
  734.2 44.3 %copy-start.48 = (f32[512]{0:T(512)S(1)}, f32[512]{0:T(512)}, u32[]{:S(2)}) copy-start(f32[512]{0:T(512)} %copy-done.47) | copy-start | bytes 6148
  (48 other events, 285.8 us)
Sparse Core Ops, SparseCore 0:
  11.4 65.4 all-gather.20
  104.1 31.2 all-gather.10
  142.4 32.8 all-gather.12
  178.6 59.7 all-gather.22
  241.1 62.9 all-gather.14
  306.7 62.6 all-gather.16
  372.2 62.6 all-gather.18
  620.5 50.5 reduce-scatter.2
  673.5 51.7 reduce-scatter.4
  731.6 573.9 all-reduce.10
